TPU v7x, 32 devices: a whole 2x2x4 slice. The times are simulated.
32 devices in a mesh: geom: 2 (over x), op: 8 (over z, y), col: 2 (over core).
Axes of the slice: x: 2, y: 2, z: 4, core: 2. Of those that a mesh axis runs over, the one named last changes fastest.
Arguments:
- wave_coef: float32 [2048, 1024], P('geom', 'col'), parts along dimension 0, may hold values from -6 to 6
- diag_energy: float32 [2048, 1024], P('geom', 'col'), parts along dimension 0, may hold values from -4 to 4
- left_block: bfloat16 [32, 1024, 1024], P(('geom', 'op')), parts along dimension 0, may hold values from -0.1875 to 0.1875
- right_block: bfloat16 [32, 1024, 1024], P(('geom', 'op'), None, 'col'), parts along dimension 0, may hold values from -0.1875 to 0.1875
- block_mask: int32 [32, 8, 8], P(('geom', 'op')), parts along dimension 0, may hold values 0 or 1
Outputs:
- new_wave: float32 [2048, 1024], P('geom', 'col'), parts along dimension 0
There are 2 independent parts, one for each index of `geom`. A program takes and returns all parts, laid end to end along the dimension named above; each array names one. Nothing has to cross between parts.
All inputs are finite; a program needn't handle non-finite values. No bound on the sum of `block_mask` on one device may be relied on, other than what follows from the above.
Results may differ from a plain program's by a relative error of at most 0.0042.
The roundings to bfloat16 on the way count: a program that leaves them out, or rounds other values in their place, can miss the bound.
Values may be sent and summed in bfloat16 or wider, within the bound.
A program may use at most 64 MiB of HBM per device.

v0:
```python
import jax
import jax.numpy as jnp
from jax import lax
from jax.sharding import PartitionSpec as P

M = 1024
STEPS = 2


def apply_mask(left_block, block_mask):
    total, width, _ = left_block.shape
    blocks = block_mask.shape[1]
    inside = width // blocks
    grid = left_block.reshape(total, blocks, inside, blocks, inside)
    keep = block_mask.astype(jnp.bfloat16)[:, :, None, :, None]
    return (grid * keep).reshape(total, width, width)


def correct(coef, sigma, diag_energy, correlation, weight, cells):
    theta = correlation / cells / (weight / cells + 1e-06)
    spacing = diag_energy - theta
    correction = (sigma - theta * coef) * spacing / jnp.maximum(spacing * spacing, 1.0)
    return coef - correction


def update_cols(coef, sigma, diag_energy, cells):
    correlation, weight = lax.psum((jnp.sum(coef * sigma), jnp.sum(coef * coef)), "col")
    moved = correct(coef, sigma, diag_energy, correlation, weight, cells)
    norm_sum = lax.psum(jnp.sum(moved * moved), "col")
    return moved * lax.rsqrt(norm_sum / cells + 1e-06)


def local(wave_coef, diag_energy, left_block, right_block, block_mask):
    masked = apply_mask(left_block, block_mask)
    cells = float(M * M)
    coef = wave_coef
    wave = wave_coef.astype(jnp.bfloat16)
    for step in range(STEPS):
        wave = coef.astype(jnp.bfloat16)
        inner = jnp.einsum(
            "mj,kjc->kmc",
            lax.all_gather(wave, "col", axis=1, tiled=True),
            right_block,
            preferred_element_type=jnp.float32,
        ).astype(jnp.bfloat16)
        partial_sum = jnp.einsum("kab,kbc->ac", masked, inner, preferred_element_type=jnp.float32)
        sigma = lax.psum(partial_sum, "op")
        coef = update_cols(coef, sigma, diag_energy, cells)
    return coef


def solution(mesh):
    in_specs = (
        P("geom", "col"),
        P("geom", "col"),
        P(("geom", "op"), None, None),
        P(("geom", "op"), None, "col"),
        P(("geom", "op"), None, None),
    )
    out_specs = P("geom", "col")
    return jax.shard_map(local, mesh=mesh, in_specs=in_specs, out_specs=out_specs, check_vma=False)
```

profile of v0, /device:TPU:0, one launch (start us, length us, event | category | flops | bytes accessed | tf_op | source)
XLA Modules:
  0.0 310.1 jit_solution(6017176165767036142)
XLA Ops:
  6.5 0.0 copy-start
  6.5 0.0 copy-start.1
  6.5 0.0 all-gather.3.cloned.1.call-start
  6.5 2.9 convert_element_type.22
  9.4 0.0 all-gather.3.cloned.1.call-update
  9.4 0.0 all-reduce.5.cloned.1.call-start
  9.5 0.0 copy-done.1
  9.5 2.5 mul.65
  12.0 7.4 %mul.66 = bf16[2,1024,1024]{2,1,0:T(8,128)(2,1)} reshape(bf16[2,8,128,8,128]{4,3,2,1,0:T(8,128)(2,1)} %mul.65) | data formatting | bytes 8388608 | tf_op jit(solution)/shard_map/mul | solution.py:16
  19.4 8.1 %mul.67 = bf16[2,1024,1024]{2,1,0:T(8,128)(2,1)} multiply(bf16[2,1024,1024]{2,1,0:T(8,128)(2,1)} %param.7, bf16[2,1024,1024]{2,1,0:T(8,128)(2,1)} %mul.66) | non-fusion elementwise | flops 2097152 | bytes 12582912 | tf_op jit(solution)/shard_map/mul | solution.py:16
  27.5 0.0 all-gather.3.cloned.1.call-done
  27.5 0.0 copy-done
  27.5 8.7 %fusion.10 = f32[1024,512]{1,0:T(8,128)} fusion(bf16[2,1024,1024]{2,1,0:T(8,128)(2,1)} %mul.67, bf16[2,1024,512]{2,1,0:T(8,128)(2,1)S(1)} %copy-done, bf16[1024,1024]{1,0:T(8,128)(2,1)} %all-gather.3.cloned.1.call-done), kind=kOutput, calls=%fused_computation.19 | convolution fusion | flops 4296015872 | bytes 10485760 | tf_op jit(solution)/shard_map/kab,kbc->ac/dot_general | solution.py:46
  36.1 0.0 all-reduce.5.cloned.1.call-update
  36.2 0.0 all-gather.5.cloned.1.call-start
  36.2 104.7 %all-reduce.5.cloned.1.call-done = f32[1024,512]{1,0:T(8,128)} async-done(((f32[1024,512]{1,0:T(8,128)}), f32[1024,512]{1,0:T(8,128)}) %all-reduce.5.cloned.1.call-update) | async-done | bytes 2097168 | tf_op jit(solution)/shard_map/psum | solution.py:47
  140.9 3.4 %multiply_reduce_fusion.4 = (f32[]{:T(128)}, f32[]{:T(128)}) fusion(f32[1024,512]{1,0:T(8,128)} %param.5, f32[1024,512]{1,0:T(8,128)} %all-reduce.5.cloned.1.call-done), kind=kLoop, calls=%fused_computation.15 | loop fusion | flops 2097150 | bytes 4194312 | tf_op jit(solution)/shard_map/reduce_sum | solution.py:27
  144.3 3.1 %all-reduce.1 = (f32[]{:T(128)}, f32[]{:T(128)}) all-reduce(f32[]{:T(128)} %get-tuple-element.8, f32[]{:T(128)} %get-tuple-element.7), channel_id=1, replica_groups=mesh['geom'=2,'op'=8,'col'=2] {'col'}, use_global_device_ids=true, to_apply=%region_2.0 | all-reduce | flops 2 | bytes 16 | tf_op jit(solution)/shard_map/psum | solution.py:27
  148.7 5.6 %multiply_reduce_fusion.3 = (f32[]{:T(128)}, f32[1024,512]{1,0:T(8,128)}) fusion(f32[1024,512]{1,0:T(8,128)} %param.5, f32[1024,512]{1,0:T(8,128)} %param.6, f32[1024,512]{1,0:T(8,128)} %all-reduce.5.cloned.1.call-done, f32[]{:T(128)S(6)} %div.32), kind=kLoop, calls=%fused_computation.13 | loop fusion | flops 5242879 | bytes 8388616 | tf_op jit(solution)/shard_map/reduce_sum | solution.py:29
  154.3 3.1 %psum.59 = f32[]{:T(128)} all-reduce(f32[]{:T(128)} %get-tuple-element.15), channel_id=1, replica_groups=mesh['geom'=2,'op'=8,'col'=2] {'col'}, use_global_device_ids=true, to_apply=%region_6.0 | all-reduce | flops 1 | bytes 8 | tf_op jit(solution)/shard_map/psum | solution.py:29
  158.1 2.8 multiply_convert_fusion
  160.9 0.0 all-gather.5.cloned.1.call-update
  160.9 0.0 all-reduce.7.cloned.1.call-start
  161.0 10.0 %all-gather.5.cloned.1.call-done = bf16[1024,1024]{1,0:T(8,128)(2,1)} async-done(((bf16[1024,512]{1,0:T(8,128)(2,1)}), bf16[1024,1024]{1,0:T(8,128)(2,1)}) %all-gather.5.cloned.1.call-update) | async-done | bytes 2097168 | tf_op jit(solution)/shard_map/all_gather | solution.py:42
  170.9 8.6 %fusion.13 = f32[1024,512]{1,0:T(8,128)} fusion(bf16[2,1024,1024]{2,1,0:T(8,128)(2,1)} %mul.67, bf16[2,1024,512]{2,1,0:T(8,128)(2,1)S(1)} %copy-done, bf16[1024,1024]{1,0:T(8,128)(2,1)} %all-gather.5.cloned.1.call-done), kind=kOutput, calls=%fused_computation.20 | convolution fusion | flops 4296015872 | bytes 10485760 | tf_op jit(solution)/shard_map/kab,kbc->ac/dot_general | solution.py:46
  179.6 0.0 all-reduce.7.cloned.1.call-update
  179.6 103.6 %all-reduce.7.cloned.1.call-done = f32[1024,512]{1,0:T(8,128)} async-done(((f32[1024,512]{1,0:T(8,128)}), f32[1024,512]{1,0:T(8,128)}) %all-reduce.7.cloned.1.call-update) | async-done | bytes 2097168 | tf_op jit(solution)/shard_map/psum | solution.py:47
  283.2 3.4 %multiply_reduce_fusion.1 = (f32[]{:T(128)}, f32[]{:T(128)}) fusion(f32[1024,512]{1,0:T(8,128)} %get-tuple-element.16, f32[]{:T(128)S(6)} %rsqrt.6, f32[1024,512]{1,0:T(8,128)} %all-reduce.7.cloned.1.call-done), kind=kLoop, calls=%fused_computation.10 | loop fusion | flops 2621438 | bytes 4194316 | tf_op jit(solution)/shard_map/reduce_sum | solution.py:27
  286.6 3.1 all-reduce
  290.9 5.6 %multiply_reduce_fusion = (f32[]{:T(128)}, f32[1024,512]{1,0:T(8,128)}) fusion(f32[1024,512]{1,0:T(8,128)} %param.6, f32[1024,512]{1,0:T(8,128)} %all-reduce.7.cloned.1.call-done, f32[]{:T(128)S(6)} %div.37, f32[1024,512]{1,0:T(8,128)} %get-tuple-element.16, f32[]{:T(128)S(6)} %rsqrt.6), kind=kLoop, calls=%fused_computation.8 | loop fusion | flops 5767167 | bytes 8388620 | tf_op jit(solution)/shard_map/reduce_sum | solution.py:29
  296.5 3.2 %psum.63 = f32[]{:T(128)} all-reduce(f32[]{:T(128)} %get-tuple-element.13), channel_id=1, replica_groups=mesh['geom'=2,'op'=8,'col'=2] {'col'}, use_global_device_ids=true, to_apply=%region_13.0 | all-reduce | flops 1 | bytes 8 | tf_op jit(solution)/shard_map/psum | solution.py:29
  300.4 3.1 %broadcast_multiply_fusion = f32[1024,512]{1,0:T(8,128)} fusion(f32[1024,512]{1,0:T(8,128)} %get-tuple-element.14, f32[]{:T(128)S(6)} %rsqrt.7), kind=kLoop, calls=%fused_computation.21 | loop fusion | flops 524288 | bytes 4194308 | tf_op jit(solution)/shard_map/mul | solution.py:30
  (1 shorter events, 0.0 us)
Async XLA Ops:
  6.5 20.9 %copy-start = (bf16[2,1024,512]{2,1,0:T(8,128)(2,1)S(1)}, bf16[2,1024,512]{2,1,0:T(8,128)(2,1)}, u32[]{:S(2)}) copy-start(bf16[2,1024,512]{2,1,0:T(8,128)(2,1)} %param.8) | copy-start | bytes 6291460
  6.5 2.9 copy-start.1
  6.5 20.9 %all-gather.3.cloned.1.call-start = ((), (), s32[]{:S(2)}) async-start(), calls=%async_computation | async-start | bytes 3145728 | tf_op jit(solution)/shard_map/all_gather | solution.py:42
  9.4 131.5 %all-reduce.5.cloned.1.call-start = ((), (), s32[]{:S(2)}) async-start(), calls=%async_computation.1 | async-start | bytes 4194304 | tf_op jit(solution)/shard_map/psum | solution.py:47
  36.2 134.8 %all-gather.5.cloned.1.call-start = ((), (), s32[]{:S(2)}) async-start(), calls=%async_computation.2 | async-start | bytes 3145728 | tf_op jit(solution)/shard_map/all_gather | solution.py:42
  160.9 122.3 %all-reduce.7.cloned.1.call-start = ((), (), s32[]{:S(2)}) async-start(), calls=%async_computation.3 | async-start | bytes 4194304 | tf_op jit(solution)/shard_map/psum | solution.py:47
Sparse Core Ops, SparseCore 0:
  9.5 13.2 all-gather.2
  36.3 104.5 all-reduce.4
  161.0 9.8 all-gather.4
  179.7 103.4 all-reduce.6
where the time goes:
time: 311 us; the launch traced here: 310 us
  waiting for transfers between devices  218 us (70%)
  other arithmetic  34.9 us (11%)
  matrix products  17.3 us (6%)
  between operations  17 us (5%)
  blocking collectives  12.5 us (4%)
  local copies, waits for them, and re-layouts  9.93 us (3%)
    psum x2, waiting for transfers between devices, local(): sigma = lax.psum(partial_sum, 'op')  208 us
    dot_general x2, matrix products, local(): jnp.einsum('kab,kbc->ac', masked, inner, preferred_element_type=jnp.float32)  17.3 us
    reduce_sum x2, other arithmetic, update_cols(): norm_sum = lax.psum(jnp.sum(moved * moved), 'col')  11.2 us
    all_gather x2, waiting for transfers between devices, local(): lax.all_gather(wave, 'col', axis=1, tiled=True)  9.96 us
    mul x2, local copies, waits for them, and re-layouts, apply_mask(): return (grid * keep).reshape(total, width, width)  9.92 us
    mul x1, other arithmetic, apply_mask(): return (grid * keep).reshape(total, width, width)  8.05 us
    reduce_sum x2, other arithmetic, update_cols(): jnp.sum(coef * coef)  6.78 us
    psum x2, blocking collectives, update_cols(): norm_sum = lax.psum(jnp.sum(moved * moved), 'col')  6.27 us
  transfers between devices with their start and end apart: 4, of which 3 were waited for; matrix products, arithmetic and copies ran while one was open for 6% of the time, Pallas kernels for 0%

commit v1 on v0

--- a/solution.py
+++ b/solution.py
@@ -1,3 +1,4 @@
+import functools
 import jax
 import jax.numpy as jnp
 from jax import lax
@@ -5,6 +6,13 @@
 
 M = 1024
 STEPS = 2
+
+
+def _wrap_samples_all(tile_in, mesh_ax):
+    return jnp.sum(lax.all_gather(tile_in, mesh_ax), axis=0)
+
+
+cover_bands = functools.partial(_wrap_samples_all, mesh_ax="op")
 
 
 def apply_mask(left_block, block_mask):
@@ -44,7 +52,7 @@
             preferred_element_type=jnp.float32,
         ).astype(jnp.bfloat16)
         partial_sum = jnp.einsum("kab,kbc->ac", masked, inner, preferred_element_type=jnp.float32)
-        sigma = lax.psum(partial_sum, "op")
+        sigma = cover_bands(partial_sum)
         coef = update_cols(coef, sigma, diag_energy, cells)
     return coef
 

time: 311 us -> 579 us (1.86)
  waiting for transfers between devices: 218 us -> 467 us
  other arithmetic: 34.9 us -> 53.9 us
    all_gather x0 -> x2, waiting for transfers between devices: none -> 458 us  [_wrap_samples_all(): return jnp.sum(lax.all_gather(tile_in, mesh_ax), axis=0)]
    psum x2 -> x0, waiting for transfers between devices: 208 us -> none  [local(): sigma = lax.psum(partial_sum, 'op')]
    reduce_sum x0 -> x2, other arithmetic: none -> 18.8 us  [_wrap_samples_all(): return jnp.sum(lax.all_gather(tile_in, mesh_ax), axis=0)]
  transfers between devices with their start and end apart: 4 -> 4, of which waited for: 3 -> 3; matrix products, arithmetic and copies ran while one was open for 6% -> 3% of each run, Pallas kernels for 0% -> 0%
where the time goes in v1:
time: 579 us; the launch traced here: 578 us
  waiting for transfers between devices  467 us (81%)
  other arithmetic  53.9 us (9%)
  matrix products  17.4 us (3%)
  between operations  17 us (3%)
  blocking collectives  12.4 us (2%)
  local copies, waits for them, and re-layouts  9.93 us (2%)
    all_gather x2, waiting for transfers between devices, _wrap_samples_all(): return jnp.sum(lax.all_gather(tile_in, mesh_ax), axis=0)  458 us
    reduce_sum x2, other arithmetic, _wrap_samples_all(): return jnp.sum(lax.all_gather(tile_in, mesh_ax), axis=0)  18.8 us
    dot_general x2, matrix products, local(): jnp.einsum('kab,kbc->ac', masked, inner, preferred_element_type=jnp.float32)  17.4 us
  transfers between devices with their start and end apart: 4, of which 3 were waited for; matrix products, arithmetic and copies ran while one was open for 3% of the time, Pallas kernels for 0%

profile of v1, /device:TPU:0, one launch (start us, length us, event | category | flops | bytes accessed | tf_op | source)
XLA Modules:
  0.0 578.0 jit_solution(5763751404830579556)
XLA Ops:
  6.5 0.0 copy-start
  6.5 0.0 copy-start.1
  6.5 0.0 all-gather.7.cloned.1.call-start
  6.5 2.9 convert_element_type.22
  9.4 0.0 all-gather.7.cloned.1.call-update
  9.4 0.0 all-gather.11.cloned.1.call-start
  9.5 0.0 copy-done.1
  9.5 2.5 mul.65
  12.0 7.4 %mul.66 = bf16[2,1024,1024]{2,1,0:T(8,128)(2,1)} reshape(bf16[2,8,128,8,128]{4,3,2,1,0:T(8,128)(2,1)} %mul.65) | data formatting | bytes 8388608 | tf_op jit(solution)/shard_map/mul | solution.py:24
  19.4 8.0 %mul.67 = bf16[2,1024,1024]{2,1,0:T(8,128)(2,1)} multiply(bf16[2,1024,1024]{2,1,0:T(8,128)(2,1)} %param.7, bf16[2,1024,1024]{2,1,0:T(8,128)(2,1)} %mul.66) | non-fusion elementwise | flops 2097152 | bytes 12582912 | tf_op jit(solution)/shard_map/mul | solution.py:24
  27.4 0.0 all-gather.7.cloned.1.call-done
  27.4 0.0 copy-done
  27.4 8.7 %fusion.10 = f32[1024,512]{1,0:T(8,128)} fusion(bf16[2,1024,1024]{2,1,0:T(8,128)(2,1)} %mul.67, bf16[2,1024,512]{2,1,0:T(8,128)(2,1)S(1)} %copy-done, bf16[1024,1024]{1,0:T(8,128)(2,1)} %all-gather.7.cloned.1.call-done), kind=kOutput, calls=%fused_computation.19 | convolution fusion | flops 4296015872 | bytes 10485760 | tf_op jit(solution)/shard_map/kab,kbc->ac/dot_general | solution.py:54
  36.1 0.0 all-gather.11.cloned.1.call-update
  36.1 0.0 all-gather.9.cloned.1.call-start
  36.2 229.7 %all-gather.11.cloned.1.call-done = f32[8192,512]{1,0:T(8,128)} async-done(((f32[1024,512]{1,0:T(8,128)}), f32[8192,512]{1,0:T(8,128)}) %all-gather.11.cloned.1.call-update) | async-done | bytes 16777232 | tf_op jit(solution)/shard_map/all_gather | solution.py:12
  265.9 9.4 %reduce_sum.72 = f32[1024,512]{1,0:T(8,128)} reduce(f32[8,1024,512]{2,1,0:T(8,128)} %bitcast.36, f32[]{:T(128)} %constant.10.clone.1), dimensions={0}, to_apply=%region_0.0 | reduce | flops 3670016 | bytes 18874372 | tf_op jit(solution)/shard_map/reduce_sum | solution.py:12
  275.3 3.4 multiply_reduce_fusion.4
  278.7 3.1 all-reduce.1
  283.2 5.7 multiply_reduce_fusion.3
  288.9 3.1 psum.44
  292.5 2.8 multiply_convert_fusion
  295.4 0.0 all-gather.9.cloned.1.call-update
  295.4 0.2 all-gather.13.cloned.1.call-start
  295.6 8.7 %all-gather.9.cloned.1.call-done = bf16[1024,1024]{1,0:T(8,128)(2,1)} async-done(((bf16[1024,512]{1,0:T(8,128)(2,1)}), bf16[1024,1024]{1,0:T(8,128)(2,1)}) %all-gather.9.cloned.1.call-update) | async-done | bytes 2097168 | tf_op jit(solution)/shard_map/all_gather | solution.py:50
  304.3 8.7 %fusion.13 = f32[1024,512]{1,0:T(8,128)} fusion(bf16[2,1024,1024]{2,1,0:T(8,128)(2,1)} %mul.67, bf16[2,1024,512]{2,1,0:T(8,128)(2,1)S(1)} %copy-done, bf16[1024,1024]{1,0:T(8,128)(2,1)} %all-gather.9.cloned.1.call-done), kind=kOutput, calls=%fused_computation.20 | convolution fusion | flops 4296015872 | bytes 10485760 | tf_op jit(solution)/shard_map/kab,kbc->ac/dot_general | solution.py:54
  313.0 0.0 all-gather.13.cloned.1.call-update
  313.0 228.6 %all-gather.13.cloned.1.call-done = f32[8192,512]{1,0:T(8,128)} async-done(((f32[1024,512]{1,0:T(8,128)}), f32[8192,512]{1,0:T(8,128)}) %all-gather.13.cloned.1.call-update) | async-done | bytes 16777232 | tf_op jit(solution)/shard_map/all_gather | solution.py:12
  541.6 9.4 %reduce_sum.76 = f32[1024,512]{1,0:T(8,128)} reduce(f32[8,1024,512]{2,1,0:T(8,128)} %bitcast.37, f32[]{:T(128)} %constant.10.clone.1), dimensions={0}, to_apply=%region_7.0 | reduce | flops 3670016 | bytes 18874372 | tf_op jit(solution)/shard_map/reduce_sum | solution.py:12
  551.1 3.4 multiply_reduce_fusion.1
  554.5 3.1 all-reduce
  559.0 5.7 multiply_reduce_fusion
  564.6 3.1 psum.47
  568.3 3.1 broadcast_multiply_fusion
  (1 shorter events, 0.0 us)
Async XLA Ops:
  6.5 20.9 %copy-start = (bf16[2,1024,512]{2,1,0:T(8,128)(2,1)S(1)}, bf16[2,1024,512]{2,1,0:T(8,128)(2,1)}, u32[]{:S(2)}) copy-start(bf16[2,1024,512]{2,1,0:T(8,128)(2,1)} %param.8) | copy-start | bytes 6291460
  6.5 2.9 copy-start.1
  6.5 20.9 %all-gather.7.cloned.1.call-start = ((), (), s32[]{:S(2)}) async-start(), calls=%async_computation | async-start | bytes 3145728 | tf_op jit(solution)/shard_map/all_gather | solution.py:50
  9.4 256.5 %all-gather.11.cloned.1.call-start = ((), (), s32[]{:S(2)}) async-start(), calls=%async_computation.2 | async-start | bytes 18874368 | tf_op jit(solution)/shard_map/all_gather | solution.py:12
  36.1 268.2 %all-gather.9.cloned.1.call-start = ((), (), s32[]{:S(2)}) async-start(), calls=%async_computation.1 | async-start | bytes 3145728 | tf_op jit(solution)/shard_map/all_gather | solution.py:50
  295.4 246.2 %all-gather.13.cloned.1.call-start = ((), (), s32[]{:S(2)}) async-start(), calls=%async_computation.3 | async-start | bytes 18874368 | tf_op jit(solution)/shard_map/all_gather | solution.py:12
Sparse Core Ops, SparseCore 0:
  9.5 13.2 all-gather.6
  36.2 229.5 all-gather.10
  295.5 8.7 all-gather.8
  313.1 228.4 all-gather.12
